TPU v7x, 32 devices: a whole 2x2x4 slice. The times are simulated.
32 devices in a mesh: groups: 2 (over y), wake: 4 (over x, core), panel: 4 (over z).
Axes of the slice: x: 2, y: 2, z: 4, core: 2. Of those that a mesh axis runs over, the one named last changes fastest.
Arguments:
- positions: float32 [3, 4096], P(None, ('groups', 'wake', 'panel')), parts along dimension 1, may hold values from -1 to 1
- strengths: float32 [3, 4096], P(None, ('groups', 'wake', 'panel')), parts along dimension 1, may hold values from -0.24 to 0.24
- cores: float32 [1, 4096], P(None, ('groups', 'wake', 'panel')), parts along dimension 1, may hold values from 0.05 to 0.2
- panel_centers: float32 [3, 32768], P(None, ('groups', 'wake', 'panel')), parts along dimension 1, may hold values from -1 to 1
- panel_normals: float32 [3, 32768], P(None, ('groups', 'wake', 'panel')), parts along dimension 1, may hold values from -1 to 1, as said below
- panel_areas: float32 [1, 32768], P(None, ('groups', 'wake', 'panel')), parts along dimension 1, may hold values from 0.004 to 0.04
- influence: float32 [32768, 16384], P(('groups', 'wake'), 'panel'), parts along dimension 0, may hold values from -1 to 2.5
- blade_ids: int32 [32768], P(('groups', 'wake', 'panel')), parts along dimension 0, may hold values from 0 to 3
- blade_velocity: float32 [8, 3], P('groups'), parts along dimension 0, may hold values from -4 to 4
Outputs:
- velocity: float32 [3, 4096], P(None, ('groups', 'wake', 'panel')), parts along dimension 1
- stretching: float32 [3, 4096], P(None, ('groups', 'wake', 'panel')), parts along dimension 1
- panel_strengths: float32 [32768], P(('groups', 'wake', 'panel')), parts along dimension 0
There are 2 independent parts, one for each index of `groups`. A program takes and returns all parts, laid end to end along the dimension named above; each array names one. Nothing has to cross between parts.
Inputs may be any that keep to these rules, and one draw needn't show every extreme that they name: `panel_normals`: each column has unit length.
All inputs are finite; a program needn't handle non-finite values.
Results may differ from a plain program's by a relative error of at most 0.0003.
Values sent between devices are 32-bit elements; how exact they have to be, the bound alone decides.
No kernel may reach another device: no remote copies, remote signals or barrier semaphores. Data moves between devices by JAX's collectives and lax.ppermute only.
A program may use at most 128 MiB of HBM per device.

v0:
```python
import math
import jax
import jax.numpy as jnp
from jax import lax
from jax.sharding import PartitionSpec as P

BLADES = 4
ITERS = 4
inv_four_pi = 1.0 / (4.0 * math.pi)
relax_factor = 0.5
freestream = (0.0, 0.0, -1.0)
block_width = 2048


def spread(block, axis, source):
    block = jnp.where(lax.axis_index(axis) == source, block, jnp.zeros_like(block))
    return lax.psum(block, axis)


def vortex_terms(targets, sources):
    target_pos, target_str, target_core = targets
    source_pos, source_str, source_core = sources
    offset_x = target_pos[0][:, None] - source_pos[0][None, :]
    offset_y = target_pos[1][:, None] - source_pos[1][None, :]
    offset_z = target_pos[2][:, None] - source_pos[2][None, :]
    core_sq = 0.5 * (
        target_core[0][:, None] * target_core[0][:, None]
        + source_core[0][None, :] * source_core[0][None, :]
    )
    distance = offset_x * offset_x + offset_y * offset_y + offset_z * offset_z + core_sq
    inverse = lax.rsqrt(distance)
    falloff = inverse * inverse * inverse
    steeper = falloff * inverse * inverse
    source_x = source_str[0][None, :]
    source_y = source_str[1][None, :]
    source_z = source_str[2][None, :]
    target_x = target_str[0][:, None]
    target_y = target_str[1][:, None]
    target_z = target_str[2][:, None]
    cross_x = offset_y * source_z - offset_z * source_y
    cross_y = offset_z * source_x - offset_x * source_z
    cross_z = offset_x * source_y - offset_y * source_x
    twist_x = target_y * source_z - target_z * source_y
    twist_y = target_z * source_x - target_x * source_z
    twist_z = target_x * source_y - target_y * source_x
    along = 3.0 * steeper * (target_x * offset_x + target_y * offset_y + target_z * offset_z)
    return jnp.stack(
        [
            jnp.sum(falloff * cross_x, axis=1),
            jnp.sum(falloff * cross_y, axis=1),
            jnp.sum(falloff * cross_z, axis=1),
            jnp.sum(falloff * twist_x - along * cross_x, axis=1),
            jnp.sum(falloff * twist_y - along * cross_y, axis=1),
            jnp.sum(falloff * twist_z - along * cross_z, axis=1),
        ]
    )


def wake_terms(targets, sources):
    points = targets[0]
    source_pos, source_str, source_core = sources
    offset_x = points[0][:, None] - source_pos[0][None, :]
    offset_y = points[1][:, None] - source_pos[1][None, :]
    offset_z = points[2][:, None] - source_pos[2][None, :]
    distance = (
        offset_x * offset_x
        + offset_y * offset_y
        + offset_z * offset_z
        + source_core[0][None, :] * source_core[0][None, :]
    )
    inverse = lax.rsqrt(distance)
    falloff = inverse * inverse * inverse
    source_x = source_str[0][None, :]
    source_y = source_str[1][None, :]
    source_z = source_str[2][None, :]
    return jnp.stack(
        [
            jnp.sum(falloff * (offset_y * source_z - offset_z * source_y), axis=1),
            jnp.sum(falloff * (offset_z * source_x - offset_x * source_z), axis=1),
            jnp.sum(falloff * (offset_x * source_y - offset_y * source_x), axis=1),
        ]
    )


def panel_terms(targets, sources):
    points = targets[0]
    centers, weights, areas = sources
    offset_x = points[0][:, None] - centers[0][None, :]
    offset_y = points[1][:, None] - centers[1][None, :]
    offset_z = points[2][:, None] - centers[2][None, :]
    distance = (
        offset_x * offset_x + offset_y * offset_y + offset_z * offset_z + 4.0 * areas[0][None, :]
    )
    inverse = lax.rsqrt(distance)
    weighted = weights[0][None, :] * inverse * inverse * inverse
    return jnp.stack(
        [
            jnp.sum(weighted * offset_x, axis=1),
            jnp.sum(weighted * offset_y, axis=1),
            jnp.sum(weighted * offset_z, axis=1),
        ]
    )


def over_sources(kernel, targets, sources, width, out_rows):
    length = sources[0].shape[-1]
    stride = math.gcd(length, width)
    if stride == length:
        return kernel(targets, sources)
    pieces = tuple(
        (
            jnp.moveaxis(source.reshape(source.shape[0], length // stride, stride), 1, 0)
            for source in sources
        )
    )

    def visit(running, entry):
        return (running + kernel(targets, entry), None)

    initial = jnp.zeros((out_rows, targets[0].shape[-1]), jnp.float32)
    running, unused = lax.scan(visit, initial, pieces)
    return running


def column_of(row_block):
    wake_count = lax.axis_size("wake")
    panel_count = lax.axis_size("panel")
    panel_at = lax.axis_index("panel")
    first_root = panel_at * wake_count // panel_count
    donors = max(1, wake_count // panel_count)
    pieces = []
    for offset_rank in range(donors):
        pieces.append(spread(row_block, "wake", first_root + offset_rank))
    joined = pieces[0] if donors == 1 else jnp.concatenate(pieces, axis=0)
    return joined


def relax(right_side, influence):
    row_side = lax.all_gather(right_side, "panel", axis=0, tiled=True)
    current = relax_factor * row_side
    for turn in range(ITERS - 1):
        column = column_of(current)
        partial_value = jnp.dot(influence, column, precision=lax.Precision.HIGHEST)
        image = lax.psum(partial_value, "panel")
        current = current + relax_factor * (row_side - image)
    own_start = lax.axis_index("panel") * right_side.shape[0]
    return lax.dynamic_slice_in_dim(current, own_start, right_side.shape[0], 0)


def per_device(
    positions,
    strengths,
    cores,
    panel_centers,
    panel_normals,
    panel_areas,
    influence,
    blade_ids,
    blade_velocity,
):
    onset_dir = jnp.asarray(freestream, jnp.float32)[:, None]
    onehot = (blade_ids[None, :] == jnp.arange(BLADES, dtype=jnp.int32)[:, None]).astype(
        jnp.float32
    )
    kinematic = jnp.dot(blade_velocity.T, onehot, precision=lax.Precision.HIGHEST) + onset_dir
    moving = -jnp.sum(panel_normals * kinematic, axis=0)
    particles = (positions, strengths, cores)
    piece = (
        lax.all_gather(positions, ("wake", "panel"), axis=1, tiled=True),
        lax.all_gather(strengths, ("wake", "panel"), axis=1, tiled=True),
        lax.all_gather(cores, ("wake", "panel"), axis=1, tiled=True),
    )
    pair_sums = over_sources(vortex_terms, particles, piece, block_width, 6)
    wake_sums = over_sources(wake_terms, (panel_centers,), piece, block_width, 3)
    right_side = moving + inv_four_pi * jnp.sum(panel_normals * wake_sums, axis=0)
    centers, areas = (
        lax.all_gather(panel_centers, ("wake", "panel"), axis=1, tiled=True),
        lax.all_gather(panel_areas, ("wake", "panel"), axis=1, tiled=True),
    )
    panel_strengths = relax(right_side, influence)
    all_strengths = lax.all_gather(panel_strengths, ("wake", "panel"), axis=0, tiled=True)
    weights = (all_strengths * areas[0])[None, :]
    panel_sums = over_sources(panel_terms, (positions,), (centers, weights, areas), block_width, 3)
    velocity = onset_dir - inv_four_pi * pair_sums[:3] + inv_four_pi * panel_sums
    stretching = -inv_four_pi * pair_sums[3:]
    return (velocity, stretching, panel_strengths)


def solution(mesh):
    in_specs = (
        P(None, ("groups", "wake", "panel")),
        P(None, ("groups", "wake", "panel")),
        P(None, ("groups", "wake", "panel")),
        P(None, ("groups", "wake", "panel")),
        P(None, ("groups", "wake", "panel")),
        P(None, ("groups", "wake", "panel")),
        P(("groups", "wake"), "panel"),
        P(("groups", "wake", "panel")),
        P("groups", None),
    )
    out_specs = (
        P(None, ("groups", "wake", "panel")),
        P(None, ("groups", "wake", "panel")),
        P(("groups", "wake", "panel")),
    )
    return jax.shard_map(
        per_device, mesh=mesh, in_specs=in_specs, out_specs=out_specs, check_vma=False
    )
```

profile of v0, /device:TPU:0, one launch (start us, length us, event | category | flops | bytes accessed | tf_op | source)
XLA Modules:
  0.0 476.9 jit_solution(10302823508321175334)
XLA Ops:
  0.6 0.0 copy-start
  0.6 0.8 slice_bitcast_fusion.3
  1.4 34.3 %all_gather.23 = f32[3,2048]{1,0:T(4,128)S(1)} all-gather(f32[3,128]{1,0:T(4,128)} %param.13), channel_id=1, replica_groups=mesh['groups'=2,'wake'=4,'panel'=4] {'wake','panel'}, dimensions={1}, use_global_device_ids=true | all-gather | bytes 26112 | tf_op jit(solution)/shard_map/all_gather | solution.py:170
  35.8 28.9 %all_gather.21 = f32[3,2048]{1,0:T(4,128)S(1)} all-gather(f32[3,128]{1,0:T(4,128)} %param.12), channel_id=1, replica_groups=mesh['groups'=2,'wake'=4,'panel'=4] {'wake','panel'}, dimensions={1}, use_global_device_ids=true | all-gather | bytes 26112 | tf_op jit(solution)/shard_map/all_gather | solution.py:169
  64.7 30.8 %all_gather.22 = f32[1,2048]{1,0:T(1,128)S(1)} all-gather(f32[1,128]{1,0:T(1,128)} %param.14), channel_id=1, replica_groups=mesh['groups'=2,'wake'=4,'panel'=4] {'wake','panel'}, dimensions={1}, use_global_device_ids=true | all-gather | bytes 8704 | tf_op jit(solution)/shard_map/all_gather | solution.py:171
  95.5 0.7 multiply_bitcast_fusion
  96.2 2.7 fusion.43
  98.9 0.8 fusion.57
  99.8 9.8 %fusion.19 = (f32[1024]{0:T(1024)S(1)}, f32[1024]{0:T(1024)S(1)}, f32[1024]{0:T(1024)S(1)}) fusion(f32[2048]{0:T(1024)S(1)} %bitcast.113, f32[2048]{0:T(1024)S(1)} %bitcast.115, f32[2048]{0:T(1024)S(1)} %bitcast.109, f32[2048]{0:T(1024)S(1)} %bitcast.119, f32[1024]{0:T(1024)S(1)} %bitcast.124, f32[2048]{0:T(1024)S(1)} %bitcast.121, f32[1024]{0:T(1024)S(1)} %bitcast.123, ...), kind=kLoop, calls=%fused_computation.45 | loop fusion | flops 54522880 | bytes 81920 | tf_op jit(solution)/shard_map/reduce_sum | solution.py:78
  109.6 0.7 fusion.49
  110.4 0.0 copy-done
  110.4 0.9 fusion.22
  111.4 13.2 %all_gather.24 = f32[4096]{0:T(1024)S(1)} all-gather(f32[1024]{0:T(1024)S(1)} %multiply_add_fusion.2), channel_id=1, replica_groups=mesh['groups'=2,'wake'=4,'panel'=4] {'panel'}, dimensions={0}, use_global_device_ids=true | all-gather | bytes 20480 | tf_op jit(solution)/shard_map/all_gather | solution.py:139
  124.6 10.2 %psum.42 = f32[4096]{0:T(1024)S(1)} all-reduce(f32[4096]{0:T(1024)S(1)} %multiply_select_fusion), channel_id=1, replica_groups=mesh['groups'=2,'wake'=4,'panel'=4] {'wake'}, use_global_device_ids=true, to_apply=%region_8.0 | all-reduce | flops 4096 | bytes 32768 | tf_op jit(solution)/shard_map/psum | solution.py:17
  134.8 58.0 %fusion.58 = f32[1,4096]{1,0:T(1,128)S(1)} fusion(f32[4096,1]{0,1:T(1,128)S(1)} %bitcast.99, f32[4096,4096]{1,0:T(8,128)} %param.18), kind=kOutput, calls=%fused_computation.117 | convolution fusion | flops 201326592 | bytes 67141632 | tf_op jit(solution)/shard_map/dot_general | solution.py:143
  192.8 15.7 %psum.43 = f32[4096]{0:T(1024)S(1)} all-reduce(f32[4096]{0:T(1024)S(1)} %bitcast.102), channel_id=1, replica_groups=mesh['groups'=2,'wake'=4,'panel'=4] {'panel'}, use_global_device_ids=true, to_apply=%region_9.0 | all-reduce | flops 4096 | bytes 32768 | tf_op jit(solution)/shard_map/psum | solution.py:144
  208.5 10.2 %psum.44 = f32[4096]{0:T(1024)S(1)} all-reduce(f32[4096]{0:T(1024)S(1)} %fusion.50), channel_id=1, replica_groups=mesh['groups'=2,'wake'=4,'panel'=4] {'wake'}, use_global_device_ids=true, to_apply=%region_10.0 | all-reduce | flops 4096 | bytes 32768 | tf_op jit(solution)/shard_map/psum | solution.py:17
  218.7 58.0 %fusion.59 = f32[1,4096]{1,0:T(1,128)S(1)} fusion(f32[4096,1]{0,1:T(1,128)S(1)} %bitcast.100, f32[4096,4096]{1,0:T(8,128)} %param.18), kind=kOutput, calls=%fused_computation.118 | convolution fusion | flops 201326592 | bytes 67141632 | tf_op jit(solution)/shard_map/dot_general | solution.py:143
  276.7 16.1 %psum.45 = f32[4096]{0:T(1024)S(1)} all-reduce(f32[4096]{0:T(1024)S(1)} %bitcast.103), channel_id=1, replica_groups=mesh['groups'=2,'wake'=4,'panel'=4] {'panel'}, use_global_device_ids=true, to_apply=%region_11.12 | all-reduce | flops 4096 | bytes 32768 | tf_op jit(solution)/shard_map/psum | solution.py:144
  292.8 10.3 %psum.46 = f32[4096]{0:T(1024)S(1)} all-reduce(f32[4096]{0:T(1024)S(1)} %get-tuple-element.85), channel_id=1, replica_groups=mesh['groups'=2,'wake'=4,'panel'=4] {'wake'}, use_global_device_ids=true, to_apply=%region_12.13 | all-reduce | flops 4096 | bytes 32768 | tf_op jit(solution)/shard_map/psum | solution.py:17
  303.2 0.0 copy-start.4
  303.2 0.0 copy-start.2
  303.2 0.0 copy-start.1
  303.2 0.0 copy-start.5
  303.2 58.0 %fusion.60 = f32[1,4096]{1,0:T(1,128)S(1)} fusion(f32[4096,1]{0,1:T(1,128)S(1)} %bitcast.101, f32[4096,4096]{1,0:T(8,128)} %param.18), kind=kOutput, calls=%fused_computation.119 | convolution fusion | flops 201326592 | bytes 67141632 | tf_op jit(solution)/shard_map/dot_general | solution.py:143
  361.2 15.8 %psum.47 = f32[4096]{0:T(1024)S(1)} all-reduce(f32[4096]{0:T(1024)S(1)} %bitcast.104), channel_id=1, replica_groups=mesh['groups'=2,'wake'=4,'panel'=4] {'panel'}, use_global_device_ids=true, to_apply=%region_13.14 | all-reduce | flops 4096 | bytes 32768 | tf_op jit(solution)/shard_map/psum | solution.py:144
  377.0 0.0 copy-start.3
  377.0 28.9 %all_gather.25 = f32[16384]{0:T(1024)S(1)} all-gather(f32[1024]{0:T(1024)S(1)} %dynamic-slice_add_fusion), channel_id=1, replica_groups=mesh['groups'=2,'wake'=4,'panel'=4] {'wake','panel'}, dimensions={0}, use_global_device_ids=true | all-gather | bytes 69632 | tf_op jit(solution)/shard_map/all_gather | solution.py:181
  406.0 0.0 copy-done.4
  406.0 31.1 %all_gather.26 = f32[1,16384]{1,0:T(1,128)S(1)} all-gather(f32[1,1024]{1,0:T(1,128)S(1)} %copy-done.4), channel_id=1, replica_groups=mesh['groups'=2,'wake'=4,'panel'=4] {'wake','panel'}, dimensions={1}, use_global_device_ids=true | all-gather | bytes 69632 | tf_op jit(solution)/shard_map/all_gather | solution.py:178
  437.1 0.0 copy-done.2
  437.1 30.7 %all_gather.27 = f32[3,16384]{1,0:T(4,128)S(1)} all-gather(f32[3,1024]{1,0:T(4,128)S(1)} %copy-done.2), channel_id=1, replica_groups=mesh['groups'=2,'wake'=4,'panel'=4] {'wake','panel'}, dimensions={1}, use_global_device_ids=true | all-gather | bytes 208896 | tf_op jit(solution)/shard_map/all_gather | solution.py:177
  467.7 0.0 copy-done.1
  467.7 7.9 %while.11 = (s32[]{:T(128)}, f32[3,128]{1,0:T(4,128)S(1)}, f32[8,1,2048]{2,1,0:T(1,128)S(1)}, f32[3,128]{1,0:T(4,128)S(1)}, f32[8,3,2048]{2,1,0:T(4,128)S(1)}, /...) while((s32[]{:T(128)}, f32[3,128]{1,0:T(4,128)S(1)}, ...), condition=%wide.region_18.19_spmd.clone, body=%wide.region_14.0_spmd.clone.sunk | while | flops 4721797 | bytes 133791 | solution.py:121
  467.8 0.9 fusion.69
  468.8 0.9 fusion.69
  469.8 0.9 fusion.69
  470.8 0.9 fusion.69
  471.8 0.9 fusion.69
  472.8 0.9 fusion.69
  473.8 0.9 fusion.69
  474.8 0.9 fusion.69
  475.7 0.0 copy-done.5
  475.7 0.7 fusion.54
  476.3 0.6 maximum_multiply_fusion.2
  476.9 0.0 copy-done.3
  (42 shorter events, 0.7 us)
Async XLA Ops:
  0.6 109.8 %copy-start = (f32[4,3]{1,0:T(4,128)S(1)}, f32[4,3]{1,0:T(4,128)}, u32[]{:S(2)}) copy-start(f32[4,3]{1,0:T(4,128)} %param.20) | copy-start | bytes 148
  303.2 102.8 %copy-start.4 = (f32[1,1024]{1,0:T(1,128)S(1)}, f32[1,1024]{1,0:T(1,128)}, u32[]{:S(2)}) copy-start(f32[1,1024]{1,0:T(1,128)} %param.17) | copy-start | bytes 12292
  303.2 133.9 %copy-start.2 = (f32[3,1024]{1,0:T(4,128)S(1)}, f32[3,1024]{1,0:T(4,128)}, u32[]{:S(2)}) copy-start(f32[3,1024]{1,0:T(4,128)} %param.15) | copy-start | bytes 36868
  303.2 164.6 %copy-start.1 = (f32[3,128]{1,0:T(4,128)S(1)}, f32[3,128]{1,0:T(4,128)}, u32[]{:S(2)}) copy-start(f32[3,128]{1,0:T(4,128)} %param.12) | copy-start | bytes 4612
  303.2 172.5 %copy-start.5 = (f32[3]{0:T(128)S(1)}, f32[3]{0:T(128)}, u32[]{:S(2)}) copy-start(f32[3]{0:T(128)} %constant.63.clone) | copy-start | bytes 40
  377.0 99.9 %copy-start.3 = (f32[1024]{0:T(1024)}, f32[1024]{0:T(1024)S(1)}, u32[]{:S(2)}) copy-start(f32[1024]{0:T(1024)S(1)} %dynamic-slice_add_fusion) | copy-start | bytes 12292
where the time goes:
time: 478 us; the launch traced here: 477 us
  blocking collectives  276 us (58%)
  matrix products  175 us (37%)
  other arithmetic  22.8 us (5%)
    dot_general x3, matrix products, relax(): partial_value = jnp.dot(influence, column, precision=lax.Precision.HIGHEST)  174 us
    psum x3, blocking collectives, relax(): image = lax.psum(partial_value, 'panel')  47.5 us
    all_gather x1, blocking collectives, per_device(): lax.all_gather(strengths, ('wake', 'panel'), axis=1, tiled=True)  34.3 us
    all_gather x1, blocking collectives, per_device(): lax.all_gather(panel_areas, ('wake', 'panel'), axis=1, tiled=True)  31.1 us
    all_gather x1, blocking collectives, per_device(): lax.all_gather(cores, ('wake', 'panel'), axis=1, tiled=True)  30.8 us
    psum x3, blocking collectives, spread(): return lax.psum(block, axis)  30.8 us
    all_gather x1, blocking collectives, per_device(): lax.all_gather(panel_centers, ('wake', 'panel'), axis=1, tiled=True)  30.7 us
    all_gather x1, blocking collectives, per_device(): lax.all_gather(panel_strengths, ('wake', 'panel'), axis=0, tiled=True)  28.9 us

commit v1 on v0

--- a/solution.py
+++ b/solution.py
@@ -168,7 +168,7 @@
     piece = (
         lax.all_gather(positions, ("wake", "panel"), axis=1, tiled=True),
         lax.all_gather(strengths, ("wake", "panel"), axis=1, tiled=True),
-        lax.all_gather(cores, ("wake", "panel"), axis=1, tiled=True),
+        jnp.concatenate(lax.all_gather(cores, ("wake", "panel")), axis=1),
     )
     pair_sums = over_sources(vortex_terms, particles, piece, block_width, 6)
     wake_sums = over_sources(wake_terms, (panel_centers,), piece, block_width, 3)

time: 478 us -> 478 us (level)
  no operation moved by 1% of the time
where the time goes in v1:
time: 478 us; the launch traced here: 477 us
  blocking collectives  276 us (58%)
  matrix products  175 us (37%)
  other arithmetic  22.8 us (5%)
    dot_general x3, matrix products, relax(): partial_value = jnp.dot(influence, column, precision=lax.Precision.HIGHEST)  174 us
    psum x3, blocking collectives, relax(): image = lax.psum(partial_value, 'panel')  47.5 us
    all_gather x1, blocking collectives, per_device(): lax.all_gather(strengths, ('wake', 'panel'), axis=1, tiled=True)  34.3 us
    all_gather x1, blocking collectives, per_device(): lax.all_gather(panel_areas, ('wake', 'panel'), axis=1, tiled=True)  31.1 us
    all_gather x1, blocking collectives, per_device(): lax.all_gather(cores, ('wake', 'panel'))  30.8 us
    psum x3, blocking collectives, spread(): return lax.psum(block, axis)  30.8 us
    all_gather x1, blocking collectives, per_device(): lax.all_gather(panel_centers, ('wake', 'panel'), axis=1, tiled=True)  30.7 us
    all_gather x1, blocking collectives, per_device(): lax.all_gather(panel_strengths, ('wake', 'panel'), axis=0, tiled=True)  28.9 us

profile of v1, /device:TPU:0, one launch (start us, length us, event | category | flops | bytes accessed | tf_op | source)
XLA Modules:
  0.0 476.9 jit_solution(5990160680350528108)
XLA Ops:
  0.6 0.0 copy-start
  0.6 0.8 slice_bitcast_fusion.3
  1.4 34.3 %all_gather.27 = f32[3,2048]{1,0:T(4,128)S(1)} all-gather(f32[3,128]{1,0:T(4,128)} %param.13), channel_id=1, replica_groups=mesh['groups'=2,'wake'=4,'panel'=4] {'wake','panel'}, dimensions={1}, use_global_device_ids=true | all-gather | bytes 26112 | tf_op jit(solution)/shard_map/all_gather | solution.py:170
  35.8 28.9 %all_gather.24 = f32[3,2048]{1,0:T(4,128)S(1)} all-gather(f32[3,128]{1,0:T(4,128)} %param.12), channel_id=1, replica_groups=mesh['groups'=2,'wake'=4,'panel'=4] {'wake','panel'}, dimensions={1}, use_global_device_ids=true | all-gather | bytes 26112 | tf_op jit(solution)/shard_map/all_gather | solution.py:169
  64.7 30.8 %all-gather.1 = f32[16,1,128]{2,1,0:T(1,128)S(1)} all-gather(f32[1,1,128]{2,1,0:T(1,128)} %bitcast.129), channel_id=2, replica_groups=mesh['groups'=2,'wake'=4,'panel'=4] {'wake','panel'}, dimensions={0}, use_global_device_ids=true | all-gather | bytes 8704 | tf_op jit(solution)/shard_map/all_gather | solution.py:171
  95.5 0.7 multiply_bitcast_fusion
  96.2 2.7 fusion.43
  98.9 0.8 fusion.57
  99.8 9.8 %fusion.19 = (f32[1024]{0:T(1024)S(1)}, f32[1024]{0:T(1024)S(1)}, f32[1024]{0:T(1024)S(1)}) fusion(f32[2048]{0:T(1024)S(1)} %bitcast.114, f32[2048]{0:T(1024)S(1)} %bitcast.116, f32[2048]{0:T(1024)S(1)} %bitcast.110, f32[2048]{0:T(1024)S(1)} %bitcast.120, f32[1024]{0:T(1024)S(1)} %bitcast.125, f32[2048]{0:T(1024)S(1)} %bitcast.122, f32[1024]{0:T(1024)S(1)} %bitcast.124, ...), kind=kLoop, calls=%fused_computation.45 | loop fusion | flops 54522880 | bytes 81920 | tf_op jit(solution)/shard_map/reduce_sum | solution.py:78
  109.6 0.7 fusion.49
  110.4 0.0 copy-done
  110.4 0.9 fusion.22
  111.4 13.2 %all_gather.28 = f32[4096]{0:T(1024)S(1)} all-gather(f32[1024]{0:T(1024)S(1)} %multiply_add_fusion.2), channel_id=1, replica_groups=mesh['groups'=2,'wake'=4,'panel'=4] {'panel'}, dimensions={0}, use_global_device_ids=true | all-gather | bytes 20480 | tf_op jit(solution)/shard_map/all_gather | solution.py:139
  124.6 10.2 %psum.42 = f32[4096]{0:T(1024)S(1)} all-reduce(f32[4096]{0:T(1024)S(1)} %multiply_select_fusion), channel_id=1, replica_groups=mesh['groups'=2,'wake'=4,'panel'=4] {'wake'}, use_global_device_ids=true, to_apply=%region_8.0 | all-reduce | flops 4096 | bytes 32768 | tf_op jit(solution)/shard_map/psum | solution.py:17
  134.8 58.0 %fusion.58 = f32[1,4096]{1,0:T(1,128)S(1)} fusion(f32[4096,1]{0,1:T(1,128)S(1)} %bitcast.100, f32[4096,4096]{1,0:T(8,128)} %param.18), kind=kOutput, calls=%fused_computation.117 | convolution fusion | flops 201326592 | bytes 67141632 | tf_op jit(solution)/shard_map/dot_general | solution.py:143
  192.8 15.7 %psum.43 = f32[4096]{0:T(1024)S(1)} all-reduce(f32[4096]{0:T(1024)S(1)} %bitcast.103), channel_id=1, replica_groups=mesh['groups'=2,'wake'=4,'panel'=4] {'panel'}, use_global_device_ids=true, to_apply=%region_9.0 | all-reduce | flops 4096 | bytes 32768 | tf_op jit(solution)/shard_map/psum | solution.py:144
  208.5 10.2 %psum.44 = f32[4096]{0:T(1024)S(1)} all-reduce(f32[4096]{0:T(1024)S(1)} %fusion.50), channel_id=1, replica_groups=mesh['groups'=2,'wake'=4,'panel'=4] {'wake'}, use_global_device_ids=true, to_apply=%region_10.0 | all-reduce | flops 4096 | bytes 32768 | tf_op jit(solution)/shard_map/psum | solution.py:17
  218.7 58.0 %fusion.59 = f32[1,4096]{1,0:T(1,128)S(1)} fusion(f32[4096,1]{0,1:T(1,128)S(1)} %bitcast.101, f32[4096,4096]{1,0:T(8,128)} %param.18), kind=kOutput, calls=%fused_computation.118 | convolution fusion | flops 201326592 | bytes 67141632 | tf_op jit(solution)/shard_map/dot_general | solution.py:143
  276.7 16.1 %psum.45 = f32[4096]{0:T(1024)S(1)} all-reduce(f32[4096]{0:T(1024)S(1)} %bitcast.104), channel_id=1, replica_groups=mesh['groups'=2,'wake'=4,'panel'=4] {'panel'}, use_global_device_ids=true, to_apply=%region_11.12 | all-reduce | flops 4096 | bytes 32768 | tf_op jit(solution)/shard_map/psum | solution.py:144
  292.8 10.3 %psum.46 = f32[4096]{0:T(1024)S(1)} all-reduce(f32[4096]{0:T(1024)S(1)} %get-tuple-element.85), channel_id=1, replica_groups=mesh['groups'=2,'wake'=4,'panel'=4] {'wake'}, use_global_device_ids=true, to_apply=%region_12.13 | all-reduce | flops 4096 | bytes 32768 | tf_op jit(solution)/shard_map/psum | solution.py:17
  303.2 0.0 copy-start.4
  303.2 0.0 copy-start.2
  303.2 0.0 copy-start.1
  303.2 0.0 copy-start.5
  303.2 58.0 %fusion.60 = f32[1,4096]{1,0:T(1,128)S(1)} fusion(f32[4096,1]{0,1:T(1,128)S(1)} %bitcast.102, f32[4096,4096]{1,0:T(8,128)} %param.18), kind=kOutput, calls=%fused_computation.119 | convolution fusion | flops 201326592 | bytes 67141632 | tf_op jit(solution)/shard_map/dot_general | solution.py:143
  361.2 15.8 %psum.47 = f32[4096]{0:T(1024)S(1)} all-reduce(f32[4096]{0:T(1024)S(1)} %bitcast.105), channel_id=1, replica_groups=mesh['groups'=2,'wake'=4,'panel'=4] {'panel'}, use_global_device_ids=true, to_apply=%region_13.14 | all-reduce | flops 4096 | bytes 32768 | tf_op jit(solution)/shard_map/psum | solution.py:144
  377.0 0.0 copy-start.3
  377.0 28.9 %all_gather.29 = f32[16384]{0:T(1024)S(1)} all-gather(f32[1024]{0:T(1024)S(1)} %dynamic-slice_add_fusion), channel_id=1, replica_groups=mesh['groups'=2,'wake'=4,'panel'=4] {'wake','panel'}, dimensions={0}, use_global_device_ids=true | all-gather | bytes 69632 | tf_op jit(solution)/shard_map/all_gather | solution.py:181
  406.0 0.0 copy-done.4
  406.0 31.1 %all_gather.30 = f32[1,16384]{1,0:T(1,128)S(1)} all-gather(f32[1,1024]{1,0:T(1,128)S(1)} %copy-done.4), channel_id=1, replica_groups=mesh['groups'=2,'wake'=4,'panel'=4] {'wake','panel'}, dimensions={1}, use_global_device_ids=true | all-gather | bytes 69632 | tf_op jit(solution)/shard_map/all_gather | solution.py:178
  437.1 0.0 copy-done.2
  437.1 30.7 %all_gather.31 = f32[3,16384]{1,0:T(4,128)S(1)} all-gather(f32[3,1024]{1,0:T(4,128)S(1)} %copy-done.2), channel_id=1, replica_groups=mesh['groups'=2,'wake'=4,'panel'=4] {'wake','panel'}, dimensions={1}, use_global_device_ids=true | all-gather | bytes 208896 | tf_op jit(solution)/shard_map/all_gather | solution.py:177
  467.7 0.0 copy-done.1
  467.7 7.9 %while.11 = (s32[]{:T(128)}, f32[3,128]{1,0:T(4,128)S(1)}, f32[8,1,2048]{2,1,0:T(1,128)S(1)}, f32[3,128]{1,0:T(4,128)S(1)}, f32[8,3,2048]{2,1,0:T(4,128)S(1)}, /...) while((s32[]{:T(128)}, f32[3,128]{1,0:T(4,128)S(1)}, ...), condition=%wide.region_18.19_spmd.clone, body=%wide.region_14.0_spmd.clone.sunk | while | flops 4721797 | bytes 133791 | solution.py:121
  467.8 0.9 fusion.69
  468.8 0.9 fusion.69
  469.8 0.9 fusion.69
  470.8 0.9 fusion.69
  471.8 0.9 fusion.69
  472.8 0.9 fusion.69
  473.8 0.9 fusion.69
  474.8 0.9 fusion.69
  475.7 0.0 copy-done.5
  475.7 0.7 fusion.54
  476.3 0.6 maximum_multiply_fusion.2
  476.9 0.0 copy-done.3
  (42 shorter events, 0.7 us)
Async XLA Ops:
  0.6 109.8 %copy-start = (f32[4,3]{1,0:T(4,128)S(1)}, f32[4,3]{1,0:T(4,128)}, u32[]{:S(2)}) copy-start(f32[4,3]{1,0:T(4,128)} %param.20) | copy-start | bytes 148
  303.2 102.8 %copy-start.4 = (f32[1,1024]{1,0:T(1,128)S(1)}, f32[1,1024]{1,0:T(1,128)}, u32[]{:S(2)}) copy-start(f32[1,1024]{1,0:T(1,128)} %param.17) | copy-start | bytes 12292
  303.2 133.9 %copy-start.2 = (f32[3,1024]{1,0:T(4,128)S(1)}, f32[3,1024]{1,0:T(4,128)}, u32[]{:S(2)}) copy-start(f32[3,1024]{1,0:T(4,128)} %param.15) | copy-start | bytes 36868
  303.2 164.6 %copy-start.1 = (f32[3,128]{1,0:T(4,128)S(1)}, f32[3,128]{1,0:T(4,128)}, u32[]{:S(2)}) copy-start(f32[3,128]{1,0:T(4,128)} %param.12) | copy-start | bytes 4612
  303.2 172.5 %copy-start.5 = (f32[3]{0:T(128)S(1)}, f32[3]{0:T(128)}, u32[]{:S(2)}) copy-start(f32[3]{0:T(128)} %constant.63.clone) | copy-start | bytes 40
  377.0 99.9 %copy-start.3 = (f32[1024]{0:T(1024)}, f32[1024]{0:T(1024)S(1)}, u32[]{:S(2)}) copy-start(f32[1024]{0:T(1024)S(1)} %dynamic-slice_add_fusion) | copy-start | bytes 12292
